TPU v7x, 256 devices: a whole 4x4x8 slice. The times are simulated.
256 devices in a mesh: doc: 8 (over z), term: 32 (over y, x, core).
Axes of the slice: x: 4, y: 4, z: 8, core: 2. Of those that a mesh axis runs over, the one named last changes fastest.
Arguments:
- tile_values: bfloat16 [8, 32, 256, 128, 128], P('doc', 'term'), may hold values from -0.03125 to 0.03125
- tile_row: int32 [8, 32, 256], P('doc', 'term'), may hold values from 0 to 31
- tile_col: int32 [8, 32, 256], P('doc', 'term'), may hold values from 0 to 31
- tile_count: int32 [8, 32], P('doc', 'term'), may hold values from 65 to 256, as said below
- targets: float32 [32, 32768], P(None, 'doc'), may hold values from -6 to 6
- ridge_weight: float32 [32], replicated, may hold values from 0.1 to 1
Outputs:
- solution: float32 [32, 131072], P(None, 'term')
- residual: float32 [32, 32768], P(None, 'doc')
- gradient: float32 [32, 131072], P(None, 'term')
Inputs may be any that keep to these rules, and one draw needn't show every extreme that they name: `tile_count`: slots at and beyond a device's count are unused; some device has all 256 slots live.
All inputs are finite; a program needn't handle non-finite values.
Results may differ from a plain program's by a relative error of at most 0.023.
Values may be sent and summed in bfloat16 or wider, within the bound.
A program may use at most 64 MiB of HBM per device.

v0:
```python
import jax
import jax.numpy as jnp
from jax import lax
from jax.sharding import PartitionSpec as P

TILE = 128
K = 32
RB = 32
CB = 32
ITERS = 2


def on_device(tile_values, tile_row, tile_col, tile_count, targets, ridge_weight):
    blocks = tile_values[0, 0]
    row_slots = tile_row[0, 0]
    col_slots = tile_col[0, 0]
    live_total = tile_count[0, 0]
    slot_total = blocks.shape[0]
    panel_size = min(32, slot_total)
    panel_count = (live_total + panel_size - 1) // panel_size

    def panel_slice(which_panel):
        first_slot = which_panel * panel_size
        tile_set = lax.dynamic_slice_in_dim(blocks, first_slot, panel_size, 0)
        row_set = lax.dynamic_slice_in_dim(row_slots, first_slot, panel_size, 0)
        col_set = lax.dynamic_slice_in_dim(col_slots, first_slot, panel_size, 0)
        alive_mask = first_slot + jnp.arange(panel_size) < live_total
        return (tile_set, row_set, col_set, alive_mask)

    def forward_part(direction):
        dir_blocks = direction.astype(jnp.bfloat16).reshape(K, CB, TILE)

        def forward_panel_step(which_panel, running):
            tile_set, row_set, col_set, alive_mask = panel_slice(which_panel)
            col_hot = (col_set[:, None] == jnp.arange(CB)[None, :]).astype(jnp.bfloat16)
            picked = jnp.einsum(
                "nc,kcb->knb", col_hot, dir_blocks, preferred_element_type=jnp.float32
            ).astype(jnp.bfloat16)
            product = jnp.einsum(
                "nab,knb->kna", tile_set, picked, preferred_element_type=jnp.float32
            )
            row_hot = jnp.logical_and(
                row_set[:, None] == jnp.arange(RB)[None, :], alive_mask[:, None]
            ).astype(jnp.float32)
            return running + jnp.einsum(
                "nr,kna->kra", row_hot, product, precision=lax.Precision.HIGHEST
            )

        running = lax.fori_loop(
            0, panel_count, forward_panel_step, jnp.zeros((K, RB, TILE), jnp.float32)
        )
        return running.reshape(K, RB * TILE)

    def adjoint_part(residual_full):
        res_blocks = residual_full.astype(jnp.bfloat16).reshape(K, RB, TILE)

        def adjoint_panel_step(which_panel, running):
            tile_set, row_set, col_set, alive_mask = panel_slice(which_panel)
            row_hot = (row_set[:, None] == jnp.arange(RB)[None, :]).astype(jnp.bfloat16)
            picked = jnp.einsum(
                "nr,kra->kna", row_hot, res_blocks, preferred_element_type=jnp.float32
            ).astype(jnp.bfloat16)
            product = jnp.einsum(
                "nab,kna->knb", tile_set, picked, preferred_element_type=jnp.float32
            )
            col_hot = jnp.logical_and(
                col_set[:, None] == jnp.arange(CB)[None, :], alive_mask[:, None]
            ).astype(jnp.float32)
            return running + jnp.einsum(
                "nc,knb->kcb", col_hot, product, precision=lax.Precision.HIGHEST
            )

        running = lax.fori_loop(
            0, panel_count, adjoint_panel_step, jnp.zeros((K, CB, TILE), jnp.float32)
        )
        return lax.psum(running.reshape(K, CB * TILE), "doc")

    def grad_norms(gradient):
        return lax.psum(jnp.sum(gradient * gradient, axis=1), "term")

    solution = jnp.zeros((K, CB * TILE), jnp.float32)
    residual_held = targets
    residual_full = targets
    gradient = adjoint_part(residual_full)
    grad_sq = grad_norms(gradient)
    direction = gradient
    dir_sq = grad_sq
    for iteration in range(ITERS):
        partial_image = forward_part(direction)
        image_rows = lax.psum(partial_image, "term")
        image_sq = lax.psum(jnp.sum(image_rows * image_rows, axis=1), "doc")
        curvature = image_sq + ridge_weight * dir_sq
        step_len = grad_sq / curvature
        solution = solution + step_len[:, None] * direction
        residual_held = residual_held - step_len[:, None] * image_rows
        residual_full = residual_held
        gradient = adjoint_part(residual_full) - ridge_weight[:, None] * solution
        if iteration + 1 < ITERS:
            new_sq = grad_norms(gradient)
            beta_ratio = new_sq / grad_sq
            direction = gradient + beta_ratio[:, None] * direction
            dir_sq = lax.psum(jnp.sum(direction * direction, axis=1), "term")
            grad_sq = new_sq
    return (solution, residual_full, gradient)


def solution(mesh):
    placed = (
        P("doc", "term", None, None, None),
        P("doc", "term", None),
        P("doc", "term", None),
        P("doc", "term"),
        P(None, "doc"),
        P(),
    )
    return jax.shard_map(
        on_device,
        mesh=mesh,
        in_specs=placed,
        out_specs=(P(None, "term"), P(None, "doc"), P(None, "term")),
        check_vma=False,
    )
```

profile of v0, /device:TPU:2, one launch (start us, length us, event | category | flops | bytes accessed | tf_op | source)
XLA Modules:
  0.0 766.1 jit_solution(4931896203188687521)
XLA Ops:
  7.9 1.1 convert_bitcast_fusion.4
  9.1 14.7 %while.50 = (s32[]{:T(128)}, f32[32,32,128]{2,1,0:T(8,128)S(1)}, s32[]{:T(128)}, s32[256]{0:T(256)}, bf16[32,32,128]{2,1,0:T(8,128)(2,1)S(1)}, /*index=5*/bf16[2...) while((s32[]{:T(128)}, f32[32,32,128]{2,1,0:T(8,128)S(1)}, ...), condition=%wide.region_1.2_spmd, body=%wide.region_0.1_spmd.sunk | while | flops 92408896 | bytes 3933175 | solution.py:73
  10.1 1.6 fusion.142
  13.2 0.8 fusion.143
  15.0 1.6 fusion.142
  20.0 1.6 fusion.142
  23.8 1.1 copy.78
  25.0 100.8 %all-reduce.6.cloned.1.call-done = f32[32,4096]{1,0:T(8,128)} async-done(((f32[32,4096]{1,0:T(8,128)}), f32[32,4096]{1,0:T(8,128)}) %all-reduce.6.cloned.1.call-update) | async-done | bytes 524304 | tf_op jit(solution)/shard_map/psum | solution.py:76
  125.8 1.4 multiply_reduce_fusion.4
  127.3 15.6 %while.51 = (s32[]{:T(128)}, f32[32,32,128]{2,1,0:T(8,128)S(1)}, s32[]{:T(128)}, s32[256]{0:T(256)}, bf16[32,32,128]{2,1,0:T(8,128)(2,1)S(1)}, /*index=5*/bf16[2...) while((s32[]{:T(128)}, f32[32,32,128]{2,1,0:T(8,128)S(1)}, ...), condition=%wide.region_6.7_spmd, body=%wide.region_5.6_spmd.sunk | while | flops 92408896 | bytes 3933175 | solution.py:49
  128.4 1.9 fusion.151
  133.6 1.9 fusion.151
  138.8 1.9 fusion.151
  142.1 0.8 fusion.152
  142.9 1.1 copy.77
  144.1 75.3 %psum.71 = f32[32]{0:T(128)S(1)} all-reduce(f32[32]{0:T(128)S(1)} %get-tuple-element.309), channel_id=1, replica_groups=mesh['doc'=8,'term'=32] {'term'}, use_global_device_ids=true, to_apply=%region_4.5 | all-reduce | flops 32 | bytes 256 | tf_op jit(solution)/shard_map/psum | solution.py:79
  219.5 61.9 %all-reduce.8.cloned.1.call-done = f32[32,4096]{1,0:T(8,128)} async-done(((f32[32,4096]{1,0:T(8,128)}), f32[32,4096]{1,0:T(8,128)}) %all-reduce.8.cloned.1.call-update) | async-done | bytes 524304 | tf_op jit(solution)/shard_map/psum | solution.py:90
  281.4 1.2 multiply_reduce_fusion.3
  282.6 17.5 %psum.73 = f32[32]{0:T(128)S(1)} all-reduce(f32[32]{0:T(128)S(1)} %multiply_reduce_fusion.3), channel_id=1, replica_groups=mesh['doc'=8,'term'=32] {'doc'}, use_global_device_ids=true, to_apply=%region_9.10 | all-reduce | flops 32 | bytes 256 | tf_op jit(solution)/shard_map/psum | solution.py:91
  300.0 1.2 convert_bitcast_fusion.2
  301.3 14.8 %while.52 = (s32[]{:T(128)}, f32[32,32,128]{2,1,0:T(8,128)S(1)}, s32[]{:T(128)}, s32[256]{0:T(256)}, bf16[32,32,128]{2,1,0:T(8,128)(2,1)S(1)}, /*index=5*/bf16[2...) while((s32[]{:T(128)}, f32[32,32,128]{2,1,0:T(8,128)S(1)}, ...), condition=%wide.region_11.12_spmd, body=%wide.region_10.11_spmd.sunk | while | flops 92408896 | bytes 3933175 | solution.py:73
  302.4 1.6 fusion.160
  307.3 1.6 fusion.160
  310.4 0.8 fusion.161
  312.3 1.6 fusion.160
  316.1 1.1 copy.76
  317.3 94.7 %all-reduce.10.cloned.1.call-done = f32[32,4096]{1,0:T(8,128)} async-done(((f32[32,4096]{1,0:T(8,128)}), f32[32,4096]{1,0:T(8,128)}) %all-reduce.10.cloned.1.call-update) | async-done | bytes 524304 | tf_op jit(solution)/shard_map/psum | solution.py:76
  412.0 1.3 multiply_reduce_fusion.2
  413.3 57.6 %psum.75 = f32[32]{0:T(128)S(1)} all-reduce(f32[32]{0:T(128)S(1)} %multiply_reduce_fusion.2), channel_id=1, replica_groups=mesh['doc'=8,'term'=32] {'term'}, use_global_device_ids=true, to_apply=%region_14.15 | all-reduce | flops 32 | bytes 256 | tf_op jit(solution)/shard_map/psum | solution.py:79
  471.0 1.3 multiply_reduce_fusion
  472.5 15.6 %while.53 = (s32[]{:T(128)}, f32[32,32,128]{2,1,0:T(8,128)S(1)}, s32[]{:T(128)}, s32[256]{0:T(256)}, bf16[32,32,128]{2,1,0:T(8,128)(2,1)S(1)}, /*index=5*/bf16[2...) while((s32[]{:T(128)}, f32[32,32,128]{2,1,0:T(8,128)S(1)}, ...), condition=%wide.region_16.17_spmd, body=%wide.region_15.16_spmd.sunk | while | flops 92408896 | bytes 3933175 | solution.py:49
  473.6 1.9 fusion.169
  478.8 1.9 fusion.169
  484.0 1.9 fusion.169
  488.1 1.1 copy.75
  489.3 78.1 %psum.78 = f32[32]{0:T(128)S(1)} all-reduce(f32[32]{0:T(128)S(1)} %get-tuple-element.307), channel_id=1, replica_groups=mesh['doc'=8,'term'=32] {'term'}, use_global_device_ids=true, to_apply=%region_21.22 | all-reduce | flops 32 | bytes 256 | tf_op jit(solution)/shard_map/psum | solution.py:102
  567.4 58.6 %all-reduce.12.cloned.1.call-done = f32[32,4096]{1,0:T(8,128)} async-done(((f32[32,4096]{1,0:T(8,128)}), f32[32,4096]{1,0:T(8,128)}) %all-reduce.12.cloned.1.call-update) | async-done | bytes 524304 | tf_op jit(solution)/shard_map/psum | solution.py:90
  625.9 1.2 multiply_reduce_fusion.1
  627.1 17.5 %psum.77 = f32[32]{0:T(128)S(1)} all-reduce(f32[32]{0:T(128)S(1)} %multiply_reduce_fusion.1), channel_id=1, replica_groups=mesh['doc'=8,'term'=32] {'doc'}, use_global_device_ids=true, to_apply=%region_19.20 | all-reduce | flops 32 | bytes 256 | tf_op jit(solution)/shard_map/psum | solution.py:91
  644.6 2.0 convert_bitcast_fusion
  646.7 14.7 %while.54 = (s32[]{:T(128)}, f32[32,32,128]{2,1,0:T(8,128)S(1)}, s32[]{:T(128)}, s32[256]{0:T(256)}, bf16[32,32,128]{2,1,0:T(8,128)(2,1)S(1)}, /*index=5*/bf16[2...) while((s32[]{:T(128)}, f32[32,32,128]{2,1,0:T(8,128)S(1)}, ...), condition=%wide.region_23.24_spmd, body=%wide.region_22.23_spmd.sunk | while | flops 92408896 | bytes 3933175 | solution.py:73
  647.8 1.6 fusion.178
  650.8 0.8 fusion.179
  652.7 1.6 fusion.178
  657.6 1.6 fusion.178
  661.5 1.1 copy.74
  662.6 94.8 %all-reduce.14.cloned.1.call-done = f32[32,4096]{1,0:T(8,128)} async-done(((f32[32,4096]{1,0:T(8,128)}), f32[32,4096]{1,0:T(8,128)}) %all-reduce.14.cloned.1.call-update) | async-done | bytes 524304 | tf_op jit(solution)/shard_map/psum | solution.py:76
  757.4 2.2 multiply_subtract_fusion
  (103 shorter events, 46.6 us)
Async XLA Ops:
  7.2 118.7 %all-reduce.6.cloned.1.call-start = ((), (), s32[]{:S(2)}) async-start(), calls=%async_computation | async-start | bytes 1048576 | tf_op jit(solution)/shard_map/psum | solution.py:76
  25.0 256.4 %all-reduce.8.cloned.1.call-start = ((), (), s32[]{:S(2)}) async-start(), calls=%async_computation.1 | async-start | bytes 1048576 | tf_op jit(solution)/shard_map/psum | solution.py:90
  127.3 172.7 %copy-start.3 = (f32[32]{0:T(128)S(1)}, f32[32]{0:T(128)}, u32[]{:S(2)}) copy-start(f32[32]{0:T(128)} %param.21) | copy-start | bytes 388
  127.3 172.7 %copy-start.1 = (f32[32,4096]{1,0:T(8,128)S(1)}, f32[32,4096]{1,0:T(8,128)}, u32[]{:S(2)}) copy-start(f32[32,4096]{1,0:T(8,128)} %param.20) | copy-start | bytes 1572868
  144.1 268.0 %all-reduce.10.cloned.1.call-start = ((), (), s32[]{:S(2)}) async-start(), calls=%async_computation.2 | async-start | bytes 1048576 | tf_op jit(solution)/shard_map/psum | solution.py:76
  301.3 110.7 %copy-start = (f32[32,4096]{1,0:T(8,128)S(1)}, f32[32,4096]{1,0:T(8,128)}, u32[]{:S(2)}) copy-start(f32[32,4096]{1,0:T(8,128)} %all-reduce.6.cloned.1.call-done) | copy-start | bytes 1572868
  317.2 308.7 %all-reduce.12.cloned.1.call-start = ((), (), s32[]{:S(2)}) async-start(), calls=%async_computation.3 | async-start | bytes 1048576 | tf_op jit(solution)/shard_map/psum | solution.py:90
  472.5 172.1 %copy-start.2 = (f32[32,4096]{1,0:T(8,128)S(1)}, f32[32,4096]{1,0:T(8,128)}, u32[]{:S(2)}) copy-start(f32[32,4096]{1,0:T(8,128)} %all-reduce.8.cloned.1.call-done) | copy-start | bytes 1572868
  489.2 268.1 %all-reduce.14.cloned.1.call-start = ((), (), s32[]{:S(2)}) async-start(), calls=%async_computation.4 | async-start | bytes 1048576 | tf_op jit(solution)/shard_map/psum | solution.py:76
Sparse Core Ops, SparseCore 0:
  25.1 100.7 all-reduce.5
  144.2 137.1 all-reduce.7
  317.4 94.6 all-reduce.9
  489.4 136.5 all-reduce.11
  662.7 94.6 all-reduce.13
where the time goes:
time: 770 us; the launch traced here: 766 us
  waiting for transfers between devices  411 us (53%)
  blocking collectives  246 us (32%)
  matrix products  42.1 us (5%)
  local copies, waits for them, and re-layouts  28.9 us (4%)
  other arithmetic  22.6 us (3%)
  between operations  14.6 us (2%)
    psum x3, waiting for transfers between devices, adjoint_part(): return lax.psum(running.reshape(K, CB * TILE), 'doc')  290 us
    psum x2, blocking collectives, grad_norms(): return lax.psum(jnp.sum(gradient * gradient, axis=1), 'term')  133 us
    psum x2, waiting for transfers between devices, on_device(): image_rows = lax.psum(partial_image, 'term')  120 us
    psum x1, blocking collectives, on_device(): dir_sq = lax.psum(jnp.sum(direction * direction, axis=1), 'term')  78.1 us
    psum x2, blocking collectives, on_device(): image_sq = lax.psum(jnp.sum(image_rows * image_rows, axis=1), 'doc')  34.9 us
  transfers between devices with their start and end apart: 5, of which 5 were waited for; matrix products, arithmetic and copies ran while one was open for 0% of the time, Pallas kernels for 0%

commit v1 on v0

v1 whole, which is shorter than its diff:
```python
import functools

import jax
import jax.numpy as jnp
from jax import lax
from jax.experimental import pallas as pl
from jax.experimental.pallas import tpu as pltpu
from jax.sharding import PartitionSpec as P

TILE = 128
K = 32
BLOCKS = 32
SLOTS = 256
UNROLL = 32
F32 = jnp.float32
BF16 = jnp.bfloat16


def slot_tables(tile_row, tile_col, tile_count):
    slot = jnp.arange(SLOTS, dtype=jnp.int32)
    live = slot < tile_count
    dest = jnp.stack([jnp.where(live, tile_col, BLOCKS), jnp.where(live, tile_row, BLOCKS)])
    source = jnp.stack([jnp.where(live, tile_row, BLOCKS), jnp.where(live, tile_col, BLOCKS)])
    order_key = dest * SLOTS + slot[None, :]
    rank = jnp.sum((order_key[:, None, :] < order_key[:, :, None]).astype(jnp.int32), axis=2)
    hit = rank[:, None, :] == slot[None, :, None]
    packed = jnp.sum(jnp.where(hit, ((dest * 64 + source) * SLOTS + slot[None, :])[:, None, :], 0), axis=2)
    perm = packed % SLOTS
    source_sorted = (packed // SLOTS) % 64
    dest_sorted = packed // (SLOTS * 64)
    same = dest_sorted[:, 1:] == dest_sorted[:, :-1]
    keep = jnp.concatenate([jnp.zeros((2, 1), F32), same.astype(F32)], axis=1)
    block = jnp.arange(BLOCKS, dtype=jnp.int32)[None, :, None]
    upto = jnp.sum((dest[:, None, :] <= block).astype(jnp.int32), axis=2)
    here = jnp.sum((dest[:, None, :] == block).astype(jnp.int32), axis=2)
    last = jnp.where(here > 0, upto - 1, SLOTS)
    return perm, source_sorted, keep, last


def sum_lanes(tile, values, base):
    lane = lax.broadcasted_iota(jnp.int32, (8, TILE), 1)
    for group in range(K // 8):
        total = jnp.sum(values[8 * group:8 * group + 8], axis=1, keepdims=True)
        tile = jnp.where(lane == base + group, total, tile)
    return tile


def per_target(tile, base):
    return jnp.concatenate([tile[:, base + g:base + g + 1] for g in range(K // 8)], axis=0)


def cgls_kernel(nd, nt, perm, source, keep, last, targets, ridge_ref, tiles_hbm,
                x_out, r_out, g_out,
                tiles, prod, vr0, vp0, vp1, vg, vq0, vq1,
                send_g, recv_g, send_q, recv_q, q_old, s_held, g_held, p_held, x_held,
                st_doc, st_term,
                tile_sem, gs_sem, gr_sem, qs_sem, qr_sem, pas_sem, par_sem, qas_sem, qar_sem,
                sds_sem, sdr_sem, sts_sem, str_sem):
    me_d = lax.axis_index("doc")
    me_t = lax.axis_index("term")
    gp = BLOCKS // nd
    qp = BLOCKS // nt
    ridge = ridge_ref[...]

    barrier = pltpu.get_barrier_semaphore()

    @pl.loop(1, nd)
    def _(o):
        pl.semaphore_signal(barrier, inc=1, device_id={"doc": lax.rem(me_d + o, nd)})

    @pl.loop(1, nt)
    def _(o):
        pl.semaphore_signal(barrier, inc=1, device_id={"term": lax.rem(me_t + o, nt)})

    load_tiles = pltpu.make_async_copy(tiles_hbm, tiles, tile_sem)
    load_tiles.start()

    zero = jnp.zeros((K, TILE), BF16)
    for v in (vr0, vp0, vp1, vq0, vq1):
        v[BLOCKS] = zero
    prod[SLOTS] = jnp.zeros((K, TILE), F32)
    for b in range(BLOCKS):
        vr0[b] = targets[:, b * TILE:(b + 1) * TILE].astype(BF16)

    def product(which, v, out, middle=None):
        def steps(first, count):
            def body(j, acc):
                for u in range(UNROLL):
                    i = j * UNROLL + u
                    tile = tiles[perm[which, i]]
                    vec = v[source[which, i]]
                    dims = (((1,), (0,)), ((), ())) if which == 0 else (((1,), (1,)), ((), ()))
                    part = lax.dot_general(vec, tile, dims, preferred_element_type=F32)
                    acc = acc * keep[which, i] + part
                    prod[i] = acc
                return acc
            return body

        half = SLOTS // UNROLL // 2
        acc = lax.fori_loop(0, half, steps(0, half), jnp.zeros((K, TILE), F32))
        if middle is not None:
            middle()
        lax.fori_loop(half, 2 * half, steps(half, half), acc)
        for b in range(BLOCKS):
            out[b] = prod[last[which, b]].astype(BF16)

    def wait_bytes(ref, sem):
        pltpu.make_async_copy(ref, ref, sem).wait()

    def scatter_g(n):
        for o in range(1, nd):
            to = lax.rem(me_d + o, nd)
            pltpu.make_async_remote_copy(
                src_ref=send_g.at[n, pl.ds(to * gp, gp)], dst_ref=recv_g.at[n, nd - 1 - o],
                send_sem=gs_sem.at[n], recv_sem=gr_sem.at[n], device_id={"doc": to}).start()

    def summed_g(n, j):
        total = prod[last[0, me_d * gp + j]]
        for s in range(nd - 1):
            total = total + recv_g[n, s, j].astype(F32)
        return total

    def gather_g(n, v):
        for o in range(1, nd):
            to = lax.rem(me_d + o, nd)
            mine = v.at[pl.ds(me_d * gp, gp)]
            pltpu.make_async_remote_copy(
                src_ref=mine, dst_ref=mine, send_sem=pas_sem.at[n], recv_sem=par_sem.at[n],
                device_id={"doc": to}).start()

    def scatter_q(n):
        @pl.loop(1, nt)
        def _(o):
            to = lax.rem(me_t + o, nt)
            pltpu.make_async_remote_copy(
                src_ref=send_q.at[n, pl.ds(to * qp, qp)], dst_ref=recv_q.at[n, nt - 1 - o],
                send_sem=qs_sem.at[n], recv_sem=qr_sem.at[n], device_id={"term": to}).start()

    def summed_q(n, j):
        total = prod[last[1, me_t * qp + j]]
        for s in range(nt - 1):
            total = total + recv_q[n, s, j].astype(F32)
        return total

    def gather_q(n, v):
        @pl.loop(1, nt)
        def _(o):
            to = lax.rem(me_t + o, nt)
            mine = v.at[pl.ds(me_t * qp, qp)]
            pltpu.make_async_remote_copy(
                src_ref=mine, dst_ref=mine, send_sem=qas_sem.at[n], recv_sem=qar_sem.at[n],
                device_id={"term": to}).start()

    def stats_doc_start(n, tile):
        st_doc[n, me_d] = tile
        for o in range(1, nd):
            to = lax.rem(me_d + o, nd)
            mine = st_doc.at[n, me_d]
            pltpu.make_async_remote_copy(
                src_ref=mine, dst_ref=mine, send_sem=sds_sem.at[n], recv_sem=sdr_sem.at[n],
                device_id={"doc": to}).start()

    def stats_doc_sum(n):
        wait_bytes(st_doc.at[n, pl.ds(0, nd - 1)], sdr_sem.at[n])
        total = st_doc[n, 0]
        for s in range(1, nd):
            total = total + st_doc[n, s]
        return total

    def stats_term_start(n, tile):
        st_term[n, me_t] = tile

        @pl.loop(1, nt)
        def _(o):
            to = lax.rem(me_t + o, nt)
            mine = st_term.at[n, me_t]
            pltpu.make_async_remote_copy(
                src_ref=mine, dst_ref=mine, send_sem=sts_sem.at[n], recv_sem=str_sem.at[n],
                device_id={"term": to}).start()

    def stats_term_sum(n):
        wait_bytes(st_term.at[n, pl.ds(0, nt - 1)], str_sem.at[n])
        total = st_term[n, 0]
        for s in range(1, nt):
            total = total + st_term[n, s]
        return total

    empty = jnp.zeros((8, TILE), F32)

    pl.semaphore_wait(barrier, nd + nt - 2)
    load_tiles.wait()

    product(0, vr0, send_g.at[0])
    scatter_g(0)
    wait_bytes(recv_g.at[0], gr_sem.at[0])
    p_sq = jnp.zeros((K, TILE), F32)
    for j in range(gp):
        total = summed_g(0, j)
        s_held[j] = total
        vp0[me_d * gp + j] = total.astype(BF16)
        p_sq = p_sq + total * total
    gather_g(0, vp0)
    wait_bytes(vp0.at[pl.ds(0, (nd - 1) * gp)], par_sem.at[0])

    product(1, vp0, send_q.at[0])
    scatter_q(0)
    wait_bytes(recv_q.at[0], qr_sem.at[0])
    q_sq = jnp.zeros((K, TILE), F32)
    for j in range(qp):
        total = summed_q(0, j)
        q_old[j] = total
        vq0[me_t * qp + j] = total.astype(BF16)
        q_sq = q_sq + total * total
    gather_q(0, vq0)
    stats_doc_start(0, sum_lanes(sum_lanes(empty, p_sq, 0), q_sq + ridge * p_sq, 4))
    wait_bytes(vq0.at[pl.ds(0, (nt - 1) * qp)], qar_sem.at[0])

    product(0, vq0, send_g.at[1], lambda: stats_term_start(0, stats_doc_sum(0)))
    scatter_g(1)
    stats = stats_term_sum(0)
    grad_sq = per_target(stats, 0)
    step0 = grad_sq / per_target(stats, 4)
    wait_bytes(recv_g.at[1], gr_sem.at[1])
    g_sq = jnp.zeros((K, TILE), F32)
    for j in range(gp):
        p = s_held[j]
        s = p - step0 * summed_g(1, j)
        x = step0 * p
        g = s - ridge * x
        p_held[j] = p
        s_held[j] = s
        x_held[j] = x
        g_held[j] = g
        vp1[me_d * gp + j] = g.astype(BF16)
        g_sq = g_sq + g * g
    gather_g(1, vp1)
    stats_term_start(1, sum_lanes(empty, g_sq, 0))
    wait_bytes(vp1.at[pl.ds(0, (nd - 1) * gp)], par_sem.at[1])

    product(1, vp1, send_q.at[1], lambda: stats_doc_start(1, stats_term_sum(1)))
    scatter_q(1)
    new_sq = per_target(stats_doc_sum(1), 0)
    beta = new_sq / grad_sq
    p_sq = jnp.zeros((K, TILE), F32)
    for j in range(gp):
        p = g_held[j] + beta * p_held[j]
        p_held[j] = p
        p_sq = p_sq + p * p
    wait_bytes(recv_q.at[1], qr_sem.at[1])
    q_sq = jnp.zeros((K, TILE), F32)
    for j in range(qp):
        total = summed_q(1, j) + beta * q_old[j]
        vq1[me_t * qp + j] = total.astype(BF16)
        q_sq = q_sq + total * total
    gather_q(1, vq1)
    stats_doc_start(2, sum_lanes(empty, q_sq + ridge * p_sq, 0))
    wait_bytes(vq1.at[pl.ds(0, (nt - 1) * qp)], qar_sem.at[1])

    product(0, vq1, send_g.at[2], lambda: stats_term_start(2, stats_doc_sum(2)))
    scatter_g(2)
    step1 = new_sq / per_target(stats_term_sum(2), 0)
    wait_bytes(recv_g.at[2], gr_sem.at[2])
    for j in range(gp):
        s = s_held[j] - step1 * summed_g(2, j)
        x = x_held[j] + step1 * p_held[j]
        vg[me_d * gp + j] = (s - ridge * x).astype(BF16)
    gather_g(2, vg)
    along0 = step0 + step1 * beta
    for b in range(BLOCKS):
        lanes = slice(b * TILE, (b + 1) * TILE)
        x_out[:, lanes] = along0 * vp0[b].astype(F32) + step1 * vp1[b].astype(F32)
        r_out[:, lanes] = (targets[:, lanes] - step0 * vq0[b].astype(F32)
                           - step1 * vq1[b].astype(F32))
    wait_bytes(vg.at[pl.ds(0, (nd - 1) * gp)], par_sem.at[2])
    for b in range(BLOCKS):
        g_out[:, b * TILE:(b + 1) * TILE] = vg[b].astype(F32)

    for n in range(3):
        wait_bytes(send_g.at[n, pl.ds(0, (nd - 1) * gp)], gs_sem.at[n])
        wait_bytes(vg.at[pl.ds(0, (nd - 1) * gp)], pas_sem.at[n])
        wait_bytes(st_doc.at[n, pl.ds(0, nd - 1)], sds_sem.at[n])
        wait_bytes(st_term.at[n, pl.ds(0, nt - 1)], sts_sem.at[n])
    for n in range(2):
        wait_bytes(send_q.at[n, pl.ds(0, (nt - 1) * qp)], qs_sem.at[n])
        wait_bytes(vq0.at[pl.ds(0, (nt - 1) * qp)], qas_sem.at[n])


def on_device(nd, nt, tile_values, tile_row, tile_col, tile_count, targets, ridge_weight):
    perm, source, keep, last = slot_tables(tile_row[0, 0], tile_col[0, 0], tile_count[0, 0])
    gp = BLOCKS // nd
    qp = BLOCKS // nt
    smem = pl.BlockSpec(memory_space=pltpu.SMEM)
    vmem = pl.BlockSpec(memory_space=pltpu.VMEM)
    dma = pltpu.SemaphoreType.DMA
    out = jax.ShapeDtypeStruct((K, BLOCKS * TILE), F32)
    vector = pltpu.VMEM((BLOCKS + 1, K, TILE), BF16)
    piece = pltpu.VMEM((gp, K, TILE), F32)
    return pl.pallas_call(
        functools.partial(cgls_kernel, nd, nt),
        out_shape=(out, out, out),
        in_specs=[smem, smem, smem, smem, vmem, vmem, pl.BlockSpec(memory_space=pl.ANY)],
        out_specs=(vmem, vmem, vmem),
        scratch_shapes=[
            pltpu.VMEM((SLOTS, TILE, TILE), BF16),
            pltpu.VMEM((SLOTS + 1, K, TILE), F32),
            vector, vector, vector, vector, vector, vector,
            pltpu.VMEM((3, BLOCKS, K, TILE), BF16),
            pltpu.VMEM((3, nd - 1, gp, K, TILE), BF16),
            pltpu.VMEM((2, BLOCKS, K, TILE), BF16),
            pltpu.VMEM((2, nt - 1, qp, K, TILE), BF16),
            pltpu.VMEM((qp, K, TILE), F32),
            piece, piece, piece, piece,
            pltpu.VMEM((3, nd, 8, TILE), F32),
            pltpu.VMEM((3, nt, 8, TILE), F32),
            dma(()), dma((3,)), dma((3,)), dma((2,)), dma((2,)), dma((3,)), dma((3,)), dma((2,)), dma((2,)),
            dma((3,)), dma((3,)), dma((3,)), dma((3,)),
        ],
        compiler_params=pltpu.CompilerParams(
            collective_id=0, has_side_effects=True, vmem_limit_bytes=48 * 1024 * 1024),
        name="cgls",
    )(perm, source, keep, last, targets, ridge_weight.reshape(K, 1), tile_values[0, 0])


def solution(mesh):
    nd, nt = mesh.shape["doc"], mesh.shape["term"]
    placed = (
        P("doc", "term", None, None, None),
        P("doc", "term", None),
        P("doc", "term", None),
        P("doc", "term"),
        P(None, "doc"),
        P(),
    )
    return jax.shard_map(
        functools.partial(on_device, nd, nt),
        mesh=mesh,
        in_specs=placed,
        out_specs=(P(None, "term"), P(None, "doc"), P(None, "term")),
        check_vma=False,
    )
```

time: 770 us -> 115 us (0.15)
  waiting for transfers between devices: 411 us -> 0 us
  blocking collectives: 246 us -> 0 us
  Pallas kernels: 0 us -> 106 us
  matrix products: 42.1 us -> 0 us
  local copies, waits for them, and re-layouts: 28.9 us -> 4.16 us
  other arithmetic: 22.6 us -> 2.17 us
  between operations: 14.6 us -> 1.31 us
    psum x5 -> x0, waiting for transfers between devices: 411 us -> none  [the longest x3 290 us: adjoint_part(): return lax.psum(running.reshape(K, CB * TILE), 'doc')]
    psum x5 -> x0, blocking collectives: 246 us -> none  [the longest x2 133 us: grad_norms(): return lax.psum(jnp.sum(gradient * gradient, axis=1), 'term')]
    pallas_call x0 -> x1, Pallas kernels: none -> 106 us  [on_device(): pl.pallas_call(functools.partial(cgls_kernel, nd, nt), out_shape=(out, ou...]
    dot_general x45 -> x0, matrix products: 42.1 us -> none  [the longest x9 14.5 us: adjoint_panel_step(): jnp.einsum('nab,kna->knb', tile_set, picked, preferred_element_type=jnp.f...]
    dynamic_slice x30 -> x0, local copies, waits for them, and re-layouts: 22.9 us -> none  [the longest x15 11.5 us: panel_slice(): row_set = lax.dynamic_slice_in_dim(row_slots, first_slot, panel_size, 0)]
    lt x15 -> x0, other arithmetic: 9.75 us -> none  [panel_slice(): alive_mask = first_slot + jnp.arange(panel_size) < live_total]
  transfers between devices with their start and end apart: 5 -> 0, of which waited for: 5 -> 0; matrix products, arithmetic and copies ran while one was open for 0% -> 0% of each run, Pallas kernels for 0% -> 0%
where the time goes in v1:
time: 115 us; the launch traced here: 114 us
  Pallas kernels  106 us (92%)
  local copies, waits for them, and re-layouts  4.16 us (4%)
  other arithmetic  2.17 us (2%)
  between operations  1.31 us (1%)
    pallas_call x1, Pallas kernels, on_device(): pl.pallas_call(functools.partial(cgls_kernel, nd, nt), out_shape=(out, ou...  106 us
    unnamed x5, local copies, waits for them, and re-layouts  3.42 us

profile of v1, /device:TPU:2, one launch (start us, length us, event | category | flops | bytes accessed | tf_op | source)
XLA Modules:
  0.0 113.7 jit_solution(2164828367693238274)
XLA Ops:
  1.3 0.7 compare_select_fusion.2
  2.0 0.7 fusion.3
  2.7 0.2 convert_reduce_fusion
  3.0 0.2 select_reduce_fusion
  3.1 0.2 convert_reduce_fusion.1
  3.3 0.1 slice_compare_fusion
  3.4 0.1 pad_convert_fusion.keep
  3.5 0.7 copy.10.ridge_ref
  4.2 0.0 copy-start
  4.2 1.0 copy-done
  5.2 106.0 %cgls.1 = (f32[32,4096]{1,0:T(8,128)S(1)}, f32[32,4096]{1,0:T(8,128)S(1)}, f32[32,4096]{1,0:T(8,128)S(1)}) custom-call(s32[2,256]{1,0:T(2,128)S(1)} %get-tuple-element.8.perm, s32[2,256]{1,0:T(2,128)S(1)} %get-tuple-element.9.source, f32[2,256]{1,0:T(2,128)S(1)} %pad_convert_fusion.keep, s32[2,32]{1,0:T(2,128)S(1)} %compare_select_fusion.6.last, ...), custom_call_target="tpu_custom_call" | custom-call | tf_op jit(solution)/shard_map/cgls/pallas_call | solution.py:298
  111.3 0.8 copy.15
  112.1 0.8 copy.16
  112.9 0.8 copy.17
  (4 shorter events, 0.1 us)
Async XLA Ops:
  4.2 1.0 copy-start

commit v2 on v0

v2 whole, which is shorter than its diff:
```python
import functools

import jax
import jax.numpy as jnp
from jax import lax
from jax.experimental import pallas as pl
from jax.experimental.pallas import tpu as pltpu
from jax.sharding import PartitionSpec as P

TILE = 128
K = 32
BLOCKS = 32
SLOTS = 256
PAIRS = (SLOTS + BLOCKS) // 2
PLACES = 384
UNROLL = 72
LOADS = 8
HALF = K // 2
HALVES = range(2)
F32 = jnp.float32
BF16 = jnp.bfloat16
INT = jnp.int32


def iota(shape, dim):
    return lax.broadcasted_iota(INT, shape, dim)


def upright(row):
    square = (row.shape[1], row.shape[1])
    return jnp.sum(jnp.where(iota(square, 0) == iota(square, 1), row, 0.0), axis=1, keepdims=True)


def slot_tables(row, col, count, table):
    slot = iota((1, SLOTS), 1).astype(F32)
    live = slot < count
    block = iota((SLOTS, TILE), 1).astype(F32)
    place = iota((SLOTS, PLACES), 1).astype(F32)
    before = iota((TILE, TILE), 0) < iota((TILE, TILE), 1)
    for which, (dest, source) in enumerate(((col, row), (row, col))):
        dest = jnp.where(live, dest, float(BLOCKS))
        code = (dest * 64.0 + jnp.where(live, source, float(BLOCKS))) * SLOTS + slot
        code_up = upright(code)
        dest_up = upright(dest)
        here = dest_up == block
        size = jnp.sum(jnp.where(here, 1.0, 0.0), axis=0, keepdims=True).astype(INT)
        padded = jnp.bitwise_and(size + 1, -2)
        start = jnp.sum(jnp.where(before, upright(padded.astype(F32)), 0.0), axis=0, keepdims=True)
        within = jnp.sum(jnp.where(jnp.logical_and(code < code_up, dest == dest_up), 1.0, 0.0),
                         axis=1, keepdims=True)
        position = within + jnp.sum(jnp.where(here, start, 0.0), axis=1, keepdims=True)
        ordered = jnp.sum(jnp.where(position == place, code_up + 1.0, 0.0), axis=0, keepdims=True)
        ordered = ordered.astype(INT) - 1
        filled = ordered >= 0
        ordered = jnp.maximum(ordered, 0)
        dest_at = jnp.right_shift(ordered, 14)
        source_at = jnp.minimum(jnp.bitwise_and(jnp.right_shift(ordered, 8), 63), BLOCKS)
        same = jnp.where(dest_at == pltpu.roll(dest_at, 2, 1), 1, 0)
        last = jnp.right_shift(start.astype(INT) + padded, 1) - 1
        last = jnp.where(size > 0, jnp.clip(last, 0, PAIRS - 1), PAIRS)
        at = 4 * which
        table[at:at + 1, :] = jnp.bitwise_and(ordered, SLOTS - 1)
        table[at + 1:at + 2, :] = jnp.where(filled, source_at, BLOCKS)
        table[at + 2:at + 3, :] = same
        for part in range(PLACES // TILE):
            table[at + 3:at + 4, part * TILE:(part + 1) * TILE] = last


def to_row(values, base):
    total = jnp.sum(values, axis=1, keepdims=True)
    here = iota((HALF, TILE), 1) == iota((HALF, TILE), 0) + base
    return jnp.sum(jnp.where(here, total, 0.0), axis=0, keepdims=True)


def from_row(row, base):
    here = iota((HALF, TILE), 1) == iota((HALF, TILE), 0) + base
    return jnp.sum(jnp.where(here, row, 0.0), axis=1, keepdims=True)


def cgls_kernel(nd, nt, info_hbm, targets_hbm, tiles_hbm,
                x_out, r_out, g_out,
                info, table_v, table, targets,
                tiles, tiles_t, prod, vectors,
                send_g, recv_g, send_q, recv_q, q_old, s_held, g_held, p_held, x_held,
                st_doc, st_term,
                info_sem, table_sem, targets_sem,
                tile_sem, gs_sem, gr_sem, qs_sem, qr_sem, pas_sem, par_sem, qas_sem, qar_sem,
                sds_sem, sdr_sem, sts_sem, str_sem):
    me_d = lax.axis_index("doc")
    me_t = lax.axis_index("term")
    gp = BLOCKS // nd
    vr0, vp0, vp1, vg, vq0, vq1 = (vectors[2 * i:2 * i + 2] for i in range(6))

    barrier = pltpu.get_barrier_semaphore()

    load_info = pltpu.make_async_copy(info_hbm, info, info_sem)
    load_info.start()
    load_targets = pltpu.make_async_copy(targets_hbm, targets, targets_sem)
    load_targets.start()
    part = SLOTS // LOADS
    load_tiles = [
        pltpu.make_async_copy(tiles_hbm.at[pl.ds(i * part, part)], tiles.at[pl.ds(i * part, part)],
                              tile_sem.at[i])
        for i in range(LOADS)
    ]
    for load in load_tiles:
        load.start()

    @pl.loop(1, nd)
    def _(o):
        pl.semaphore_signal(barrier, inc=1, device_id={"doc": lax.rem(me_d + o, nd)})

    @pl.loop(1, nt)
    def _(o):
        pl.semaphore_signal(barrier, inc=1, device_id={"term": lax.rem(me_t + o, nt)})

    zero = jnp.zeros((HALF, TILE), BF16)
    for h in HALVES:
        for v in (vr0, vp0, vp1, vq0, vq1):
            v[h][BLOCKS] = zero
        prod[h, PAIRS] = jnp.zeros((HALF, TILE), F32)

    load_info.wait()
    slot_tables(info[0:1, :], info[1:2, :], info[2:3, :], table_v)
    move_table = pltpu.make_async_copy(table_v, table, table_sem)
    move_table.start()
    ridge_all = upright(info[3:4, :TILE])
    ridge = [ridge_all[h * HALF:(h + 1) * HALF] for h in HALVES]
    load_targets.wait()
    for b in range(BLOCKS):
        for h in HALVES:
            vr0[h][b] = targets[h * HALF:(h + 1) * HALF, b * TILE:(b + 1) * TILE].astype(BF16)
    move_table.wait()
    for load in load_tiles:
        load.wait()

    def product(which, v, h):
        matrix = tiles if which == 0 else tiles_t
        at = 4 * which

        def body(j, acc):
            for u in range(UNROLL):
                i = j * UNROLL + u
                left = jnp.concatenate([v[h][table[at + 1, 2 * i + e]] for e in range(2)], axis=1)
                right = jnp.concatenate([matrix[table[at, 2 * i + e]] for e in range(2)], axis=0)
                acc = (acc * table[at + 2, 2 * i].astype(F32)
                       + jnp.dot(left, right, preferred_element_type=F32))
                prod[h, i] = acc
            return acc

        lax.fori_loop(0, PAIRS // UNROLL, body, jnp.zeros((HALF, TILE), F32))

    def product_block(which, h, b):
        return prod[h, table[4 * which + 3, b]]

    def wait_bytes(ref, sem):
        pltpu.make_async_copy(ref, ref, sem).wait()

    doc_far = sorted(range(1, nd), key=lambda o: -min(o, nd - o))
    ny, nx = nt // 8, 4
    term_far = sorted(
        ((y, x, c) for y in range(ny) for x in range(nx) for c in range(2) if (y, x, c) != (0, 0, 0)),
        key=lambda o: -(min(o[0], ny - o[0]) + min(o[1], nx - o[1])))

    def doc_peer(o):
        return lax.rem(me_d + o, nd)

    def term_peer(o):
        y = lax.rem(me_t // (2 * nx) + o[0], ny)
        x = lax.rem(lax.rem(me_t // 2, nx) + o[1], nx)
        c = lax.rem(me_t + o[2], 2)
        return (y * nx + x) * 2 + c

    def scatter_g(n, h):
        for b in range(BLOCKS):
            send_g[n, h, b] = product_block(0, h, b).astype(BF16)
        for i, o in enumerate(doc_far):
            to = doc_peer(o)
            pltpu.make_async_remote_copy(
                src_ref=send_g.at[n, h, pl.ds(to * gp, gp)], dst_ref=recv_g.at[n, h, i],
                send_sem=gs_sem.at[n, h], recv_sem=gr_sem.at[n, h], device_id={"doc": to}).start()

    def scattered_g(n, h):
        wait_bytes(recv_g.at[n, h], gr_sem.at[n, h])

    def summed_g(n, h, j):
        total = product_block(0, h, me_d * gp + j)
        for s in range(nd - 1):
            total = total + recv_g[n, h, s, j].astype(F32)
        return total

    def gather_g(n, h, v):
        for o in doc_far:
            mine = v[h].at[pl.ds(me_d * gp, gp)]
            pltpu.make_async_remote_copy(
                src_ref=mine, dst_ref=mine, send_sem=pas_sem.at[n, h], recv_sem=par_sem.at[n, h],
                device_id={"doc": doc_peer(o)}).start()

    def gathered_g(n, h, v):
        wait_bytes(v[h].at[pl.ds(0, (nd - 1) * gp)], par_sem.at[n, h])

    def scatter_q(n, h):
        for b in range(BLOCKS):
            send_q[n, h, b] = product_block(1, h, b).astype(BF16)
        for i, o in enumerate(term_far):
            to = term_peer(o)
            pltpu.make_async_remote_copy(
                src_ref=send_q.at[n, h, to], dst_ref=recv_q.at[n, h, i],
                send_sem=qs_sem.at[n, h], recv_sem=qr_sem.at[n, h], device_id={"term": to}).start()

    def summed_q(n, h):
        wait_bytes(recv_q.at[n, h], qr_sem.at[n, h])
        total = product_block(1, h, me_t)
        for s in range(nt - 1):
            total = total + recv_q[n, h, s].astype(F32)
        return total

    def gather_q(n, h, v, piece):
        v[h][me_t] = piece.astype(BF16)
        for o in term_far:
            mine = v[h].at[me_t]
            pltpu.make_async_remote_copy(
                src_ref=mine, dst_ref=mine, send_sem=qas_sem.at[n, h], recv_sem=qar_sem.at[n, h],
                device_id={"term": term_peer(o)}).start()

    def gathered_q(n, h, v):
        wait_bytes(v[h].at[pl.ds(0, nt - 1)], qar_sem.at[n, h])

    def stats_start(n, row):
        st_term[n, me_t] = row

        @pl.loop(1, nt)
        def _(o):
            mine = st_term.at[n, me_t]
            pltpu.make_async_remote_copy(
                src_ref=mine, dst_ref=mine, send_sem=sts_sem.at[n], recv_sem=str_sem.at[n],
                device_id={"term": lax.rem(me_t + o, nt)}).start()

    def stats_turn(n):
        wait_bytes(st_term.at[n, pl.ds(0, nt - 1)], str_sem.at[n])
        total = st_term[n, 0]
        for s in range(1, nt):
            total = total + st_term[n, s]
        st_doc[n, me_d] = total
        for o in doc_far:
            mine = st_doc.at[n, me_d]
            pltpu.make_async_remote_copy(
                src_ref=mine, dst_ref=mine, send_sem=sds_sem.at[n], recv_sem=sdr_sem.at[n],
                device_id={"doc": doc_peer(o)}).start()

    def stats_end(n):
        wait_bytes(st_doc.at[n, pl.ds(0, nd - 1)], sdr_sem.at[n])
        total = st_doc[n, 0]
        for s in range(1, nd):
            total = total + st_doc[n, s]
        return total

    nothing = jnp.zeros((HALF, TILE), F32)

    for h in HALVES:
        product(0, vr0, h)
    pl.semaphore_wait(barrier, nd + nt - 2)
    for h in HALVES:
        scatter_g(0, h)

    @pl.loop(0, SLOTS // 32)
    def _(j):
        for u in range(32):
            tiles_t[j * 32 + u] = tiles[j * 32 + u].T

    p_sq = [nothing, nothing]
    for h in HALVES:
        scattered_g(0, h)
        for j in range(gp):
            total = summed_g(0, h, j)
            vp0[h][me_d * gp + j] = total.astype(BF16)
            s_held[h, j] = total
            p_sq[h] = p_sq[h] + total * total
        gather_g(0, h, vp0)

    for h in HALVES:
        gathered_g(0, h, vp0)
        product(1, vp0, h)
        scatter_q(0, h)
    row = jnp.zeros((1, TILE), F32)
    for h in HALVES:
        total = summed_q(0, h)
        gather_q(0, h, vq0, total)
        q_old[h] = total
        row = row + to_row(p_sq[h], h * HALF) + to_row(total * total + ridge[h] * p_sq[h], K + h * HALF)
    stats_start(0, row)

    for h in HALVES:
        gathered_q(0, h, vq0)
        product(0, vq0, h)
        scatter_g(1, h)
        if h == 0:
            stats_turn(0)
    stats = stats_end(0)
    grad_sq = [from_row(stats, h * HALF) for h in HALVES]
    step0 = [grad_sq[h] / from_row(stats, K + h * HALF) for h in HALVES]
    row = jnp.zeros((1, TILE), F32)
    for h in HALVES:
        scattered_g(1, h)
        g_sq = nothing
        for j in range(gp):
            p = s_held[h, j]
            x = step0[h] * p
            s = p - step0[h] * summed_g(1, h, j)
            g = s - ridge[h] * x
            vp1[h][me_d * gp + j] = g.astype(BF16)
            p_held[h, j] = p
            s_held[h, j] = s
            x_held[h, j] = x
            g_held[h, j] = g
            g_sq = g_sq + g * g
        gather_g(1, h, vp1)
        row = row + to_row(g_sq, h * HALF)
    stats_start(1, row)

    for h in HALVES:
        gathered_g(1, h, vp1)
        product(1, vp1, h)
        scatter_q(1, h)
        if h == 0:
            stats_turn(1)
    stats = stats_end(1)
    new_sq = [from_row(stats, h * HALF) for h in HALVES]
    beta = [new_sq[h] / grad_sq[h] for h in HALVES]
    row = jnp.zeros((1, TILE), F32)
    for h in HALVES:
        total = summed_q(1, h) + beta[h] * q_old[h]
        gather_q(1, h, vq1, total)
        p_sq = nothing
        for j in range(gp):
            p = g_held[h, j] + beta[h] * p_held[h, j]
            p_held[h, j] = p
            p_sq = p_sq + p * p
        row = row + to_row(total * total + ridge[h] * p_sq, h * HALF)
    stats_start(2, row)

    for h in HALVES:
        gathered_q(1, h, vq1)
        product(0, vq1, h)
        scatter_g(2, h)
        if h == 0:
            stats_turn(2)
    stats = stats_end(2)
    step1 = [new_sq[h] / from_row(stats, h * HALF) for h in HALVES]
    for h in HALVES:
        scattered_g(2, h)
        for j in range(gp):
            x = x_held[h, j] + step1[h] * p_held[h, j]
            s = s_held[h, j] - step1[h] * summed_g(2, h, j)
            vg[h][me_d * gp + j] = (s - ridge[h] * x).astype(BF16)
        gather_g(2, h, vg)
    for h in HALVES:
        rows = slice(h * HALF, (h + 1) * HALF)
        along0 = step0[h] + step1[h] * beta[h]
        for b in range(BLOCKS):
            lanes = slice(b * TILE, (b + 1) * TILE)
            x_out[rows, lanes] = along0 * vp0[h][b].astype(F32) + step1[h] * vp1[h][b].astype(F32)
            r_out[rows, lanes] = (targets[rows, lanes] - step0[h] * vq0[h][b].astype(F32)
                                  - step1[h] * vq1[h][b].astype(F32))
    for h in HALVES:
        gathered_g(2, h, vg)
        for b in range(BLOCKS):
            g_out[h * HALF:(h + 1) * HALF, b * TILE:(b + 1) * TILE] = vg[h][b].astype(F32)

    for n in range(3):
        for h in HALVES:
            wait_bytes(vg[h].at[pl.ds(0, (nd - 1) * gp)], gs_sem.at[n, h])
            wait_bytes(vg[h].at[pl.ds(0, (nd - 1) * gp)], pas_sem.at[n, h])
        wait_bytes(st_doc.at[n, pl.ds(0, nd - 1)], sds_sem.at[n])
        wait_bytes(st_term.at[n, pl.ds(0, nt - 1)], sts_sem.at[n])
    for n in range(2):
        for h in HALVES:
            wait_bytes(vq0[h].at[pl.ds(0, nt - 1)], qs_sem.at[n, h])
            wait_bytes(vq0[h].at[pl.ds(0, nt - 1)], qas_sem.at[n, h])


def store_kernel(x, r, g, x_out, r_out, g_out, sems):
    copies = [pltpu.make_async_copy(a, b, sems.at[i])
              for i, (a, b) in enumerate(((x, x_out), (r, r_out), (g, g_out)))]
    for copy in copies:
        copy.start()
    for copy in copies:
        copy.wait()


def on_device(nd, nt, tile_values, tile_row, tile_col, tile_count, targets, ridge_weight):
    gp = BLOCKS // nd
    hbm = pl.BlockSpec(memory_space=pl.ANY)
    vmem = pl.BlockSpec(memory_space=pltpu.VMEM)
    dma = pltpu.SemaphoreType.DMA
    out = jax.ShapeDtypeStruct((K, BLOCKS * TILE), F32)
    vector = pltpu.VMEM((BLOCKS + 1, HALF, TILE), BF16)
    piece = pltpu.VMEM((2, gp, HALF, TILE), F32)
    matrix = pltpu.VMEM((SLOTS, TILE, TILE), BF16)
    info = jnp.concatenate([
        tile_row.reshape(1, SLOTS).astype(F32),
        tile_col.reshape(1, SLOTS).astype(F32),
        jnp.broadcast_to(tile_count.astype(F32), (1, SLOTS)),
        jnp.pad(ridge_weight, (0, SLOTS - K)).reshape(1, SLOTS),
    ], axis=0)
    results = pl.pallas_call(
        functools.partial(cgls_kernel, nd, nt),
        out_shape=(out, out, out),
        in_specs=[hbm] * 3,
        out_specs=(vmem, vmem, vmem),
        scratch_shapes=[
            pltpu.VMEM((4, SLOTS), F32),
            pltpu.VMEM((8, PLACES), INT), pltpu.SMEM((8, PLACES), INT),
            pltpu.VMEM((K, BLOCKS * TILE), F32),
            matrix, matrix,
            pltpu.VMEM((2, PAIRS + 1, HALF, TILE), F32),
            [vector] * 12,
            pltpu.VMEM((3, 2, BLOCKS, HALF, TILE), BF16),
            pltpu.VMEM((3, 2, nd - 1, gp, HALF, TILE), BF16),
            pltpu.VMEM((2, 2, BLOCKS, HALF, TILE), BF16),
            pltpu.VMEM((2, 2, nt - 1, HALF, TILE), BF16),
            pltpu.VMEM((2, HALF, TILE), F32),
            piece, piece, piece, piece,
            pltpu.VMEM((3, nd, 1, TILE), F32),
            pltpu.VMEM((3, nt, 1, TILE), F32),
            dma(()), dma(()), dma(()),
            dma((LOADS,)), dma((3, 2)), dma((3, 2)), dma((2, 2)), dma((2, 2)),
            dma((3, 2)), dma((3, 2)), dma((2, 2)), dma((2, 2)),
            dma((3,)), dma((3,)), dma((3,)), dma((3,)),
        ],
        compiler_params=pltpu.CompilerParams(
            collective_id=0, has_side_effects=True, vmem_limit_bytes=48 * 1024 * 1024),
        name="cgls",
    )(info, targets, tile_values[0, 0])
    return pl.pallas_call(
        store_kernel,
        out_shape=(out, out, out),
        in_specs=[vmem] * 3,
        out_specs=(hbm, hbm, hbm),
        scratch_shapes=[dma((3,))],
        compiler_params=pltpu.CompilerParams(vmem_limit_bytes=2 * 1024 * 1024),
        name="store",
    )(*results)


def solution(mesh):
    nd, nt = mesh.shape["doc"], mesh.shape["term"]
    placed = (
        P("doc", "term", None, None, None),
        P("doc", "term", None),
        P("doc", "term", None),
        P("doc", "term"),
        P(None, "doc"),
        P(),
    )
    return jax.shard_map(
        functools.partial(on_device, nd, nt),
        mesh=mesh,
        in_specs=placed,
        out_specs=(P(None, "term"), P(None, "doc"), P(None, "term")),
        check_vma=False,
    )
```

time: 770 us -> 84.4 us (0.11)
  waiting for transfers between devices: 411 us -> 0 us
  blocking collectives: 246 us -> 0 us
  Pallas kernels: 0 us -> 80.3 us
  matrix products: 42.1 us -> 0 us
  local copies, waits for them, and re-layouts: 28.9 us -> 1.77 us
  other arithmetic: 22.6 us -> 0.77 us
  between operations: 14.6 us -> 1.29 us
    psum x5 -> x0, waiting for transfers between devices: 411 us -> none  [the longest x3 290 us: adjoint_part(): return lax.psum(running.reshape(K, CB * TILE), 'doc')]
    psum x5 -> x0, blocking collectives: 246 us -> none  [the longest x2 133 us: grad_norms(): return lax.psum(jnp.sum(gradient * gradient, axis=1), 'term')]
    pallas_call x0 -> x2, Pallas kernels: none -> 80.3 us  [the longest x1 79.1 us: on_device(): pl.pallas_call(functools.partial(cgls_kernel, nd, nt), out_shape=(out, ou...]
    dot_general x45 -> x0, matrix products: 42.1 us -> none  [the longest x9 14.5 us: adjoint_panel_step(): jnp.einsum('nab,kna->knb', tile_set, picked, preferred_element_type=jnp.f...]
    dynamic_slice x30 -> x0, local copies, waits for them, and re-layouts: 22.9 us -> none  [the longest x15 11.5 us: panel_slice(): row_set = lax.dynamic_slice_in_dim(row_slots, first_slot, panel_size, 0)]
    lt x15 -> x0, other arithmetic: 9.75 us -> none  [panel_slice(): alive_mask = first_slot + jnp.arange(panel_size) < live_total]
  transfers between devices with their start and end apart: 5 -> 0, of which waited for: 5 -> 0; matrix products, arithmetic and copies ran while one was open for 0% -> 0% of each run, Pallas kernels for 0% -> 0%
where the time goes in v2:
time: 84.4 us; the launch traced here: 84.1 us
  Pallas kernels  80.3 us (95%)
  local copies, waits for them, and re-layouts  1.77 us (2%)
  between operations  1.29 us (2%)
    pallas_call x1, Pallas kernels, on_device(): pl.pallas_call(functools.partial(cgls_kernel, nd, nt), out_shape=(out, ou...  79.1 us

profile of v2, /device:TPU:2, one launch (start us, length us, event | category | flops | bytes accessed | tf_op | source)
XLA Modules:
  0.0 84.1 jit_solution(2740169673582306272)
XLA Ops:
  1.3 0.1 pad.7.clone
  1.4 0.7 pad.4
  2.0 0.7 convert_bitcast_fusion
  2.7 0.1 pad_maximum_fusion.info_hbm
  2.8 0.0 copy-start
  2.8 1.0 %copy-done = f32[32,4096]{1,0:T(8,128)S(1)} copy-done((f32[32,4096]{1,0:T(8,128)S(1)}, f32[32,4096]{1,0:T(8,128)}, u32[]{:S(2)}) %copy-start) | copy-done | bytes 524312
  3.8 79.1 %cgls.1 = (f32[32,4096]{1,0:T(8,128)S(1)}, f32[32,4096]{1,0:T(8,128)S(1)}, f32[32,4096]{1,0:T(8,128)S(1)}) custom-call(f32[4,256]{1,0:T(4,128)S(1)} %pad_maximum_fusion.info_hbm, f32[32,4096]{1,0:T(8,128)S(1)} %copy-done, bf16[256,128,128]{2,1,0:T(8,128)(2,1)} %bitcast.9), custom_call_target="tpu_custom_call" | custom-call | tf_op jit(solution)/shard_map/cgls/pallas_call | solution.py:406
  83.0 1.2 %store.1 = (f32[32,4096]{1,0:T(8,128)}, f32[32,4096]{1,0:T(8,128)}, f32[32,4096]{1,0:T(8,128)}) custom-call(f32[32,4096]{1,0:T(8,128)S(1)} %get-tuple-element.6.x, f32[32,4096]{1,0:T(8,128)S(1)} %get-tuple-element.7.r, f32[32,4096]{1,0:T(8,128)S(1)} %get-tuple-element.8.g), custom_call_target="tpu_custom_call" | custom-call | tf_op jit(solution)/shard_map/store/pallas_call | solution.py:435
Async XLA Ops:
  2.8 1.0 %copy-start = (f32[32,4096]{1,0:T(8,128)S(1)}, f32[32,4096]{1,0:T(8,128)}, u32[]{:S(2)}) copy-start(f32[32,4096]{1,0:T(8,128)} %targets_hbm.1) | copy-start | bytes 1572868

commit v3 on v2

--- a/solution.py
+++ b/solution.py
@@ -31,39 +31,36 @@
     return jnp.sum(jnp.where(iota(square, 0) == iota(square, 1), row, 0.0), axis=1, keepdims=True)
 
 
-def slot_tables(row, col, count, table):
+def slot_table(dest, source, live, table):
     slot = iota((1, SLOTS), 1).astype(F32)
-    live = slot < count
     block = iota((SLOTS, TILE), 1).astype(F32)
     place = iota((SLOTS, PLACES), 1).astype(F32)
     before = iota((TILE, TILE), 0) < iota((TILE, TILE), 1)
-    for which, (dest, source) in enumerate(((col, row), (row, col))):
-        dest = jnp.where(live, dest, float(BLOCKS))
-        code = (dest * 64.0 + jnp.where(live, source, float(BLOCKS))) * SLOTS + slot
-        code_up = upright(code)
-        dest_up = upright(dest)
-        here = dest_up == block
-        size = jnp.sum(jnp.where(here, 1.0, 0.0), axis=0, keepdims=True).astype(INT)
-        padded = jnp.bitwise_and(size + 1, -2)
-        start = jnp.sum(jnp.where(before, upright(padded.astype(F32)), 0.0), axis=0, keepdims=True)
-        within = jnp.sum(jnp.where(jnp.logical_and(code < code_up, dest == dest_up), 1.0, 0.0),
-                         axis=1, keepdims=True)
-        position = within + jnp.sum(jnp.where(here, start, 0.0), axis=1, keepdims=True)
-        ordered = jnp.sum(jnp.where(position == place, code_up + 1.0, 0.0), axis=0, keepdims=True)
-        ordered = ordered.astype(INT) - 1
-        filled = ordered >= 0
-        ordered = jnp.maximum(ordered, 0)
-        dest_at = jnp.right_shift(ordered, 14)
-        source_at = jnp.minimum(jnp.bitwise_and(jnp.right_shift(ordered, 8), 63), BLOCKS)
-        same = jnp.where(dest_at == pltpu.roll(dest_at, 2, 1), 1, 0)
-        last = jnp.right_shift(start.astype(INT) + padded, 1) - 1
-        last = jnp.where(size > 0, jnp.clip(last, 0, PAIRS - 1), PAIRS)
-        at = 4 * which
-        table[at:at + 1, :] = jnp.bitwise_and(ordered, SLOTS - 1)
-        table[at + 1:at + 2, :] = jnp.where(filled, source_at, BLOCKS)
-        table[at + 2:at + 3, :] = same
-        for part in range(PLACES // TILE):
-            table[at + 3:at + 4, part * TILE:(part + 1) * TILE] = last
+    dest = jnp.where(live, dest, float(BLOCKS))
+    code = (dest * 64.0 + jnp.where(live, source, float(BLOCKS))) * SLOTS + slot
+    code_up = upright(code)
+    dest_up = upright(dest)
+    here = dest_up == block
+    size = jnp.sum(jnp.where(here, 1.0, 0.0), axis=0, keepdims=True).astype(INT)
+    padded = jnp.bitwise_and(size + 1, -2)
+    start = jnp.sum(jnp.where(before, upright(padded.astype(F32)), 0.0), axis=0, keepdims=True)
+    within = jnp.sum(jnp.where(jnp.logical_and(code < code_up, dest == dest_up), 1.0, 0.0),
+                     axis=1, keepdims=True)
+    position = within + jnp.sum(jnp.where(here, start, 0.0), axis=1, keepdims=True)
+    ordered = jnp.sum(jnp.where(position == place, code_up + 1.0, 0.0), axis=0, keepdims=True)
+    ordered = ordered.astype(INT) - 1
+    filled = ordered >= 0
+    ordered = jnp.maximum(ordered, 0)
+    dest_at = jnp.right_shift(ordered, 14)
+    source_at = jnp.minimum(jnp.bitwise_and(jnp.right_shift(ordered, 8), 63), BLOCKS)
+    same = jnp.where(dest_at == pltpu.roll(dest_at, 2, 1), 1, 0)
+    last = jnp.right_shift(start.astype(INT) + padded, 1) - 1
+    last = jnp.where(size > 0, jnp.clip(last, 0, PAIRS - 1), PAIRS)
+    table[0:1, :] = jnp.bitwise_and(ordered, SLOTS - 1)
+    table[1:2, :] = jnp.where(filled, source_at, BLOCKS)
+    table[2:3, :] = same
+    for part in range(PLACES // TILE):
+        table[3:4, part * TILE:(part + 1) * TILE] = last
 
 
 def to_row(values, base):
@@ -77,13 +74,13 @@
     return jnp.sum(jnp.where(here, row, 0.0), axis=1, keepdims=True)
 
 
-def cgls_kernel(nd, nt, info_hbm, targets_hbm, tiles_hbm,
+def cgls_kernel(nd, nt, places, ridge_smem, targets_hbm, tiles_hbm,
                 x_out, r_out, g_out,
-                info, table_v, table, targets,
+                tables_v, tables, targets,
                 tiles, tiles_t, prod, vectors,
                 send_g, recv_g, send_q, recv_q, q_old, s_held, g_held, p_held, x_held,
                 st_doc, st_term,
-                info_sem, table_sem, targets_sem,
+                table_sem, targets_sem,
                 tile_sem, gs_sem, gr_sem, qs_sem, qr_sem, pas_sem, par_sem, qas_sem, qar_sem,
                 sds_sem, sdr_sem, sts_sem, str_sem):
     me_d = lax.axis_index("doc")
@@ -93,8 +90,6 @@
 
     barrier = pltpu.get_barrier_semaphore()
 
-    load_info = pltpu.make_async_copy(info_hbm, info, info_sem)
-    load_info.start()
     load_targets = pltpu.make_async_copy(targets_hbm, targets, targets_sem)
     load_targets.start()
     part = SLOTS // LOADS
@@ -120,12 +115,21 @@
             v[h][BLOCKS] = zero
         prod[h, PAIRS] = jnp.zeros((HALF, TILE), F32)
 
-    load_info.wait()
-    slot_tables(info[0:1, :], info[1:2, :], info[2:3, :], table_v)
-    move_table = pltpu.make_async_copy(table_v, table, table_sem)
-    move_table.start()
-    ridge_all = upright(info[3:4, :TILE])
-    ridge = [ridge_all[h * HALF:(h + 1) * HALF] for h in HALVES]
+    def build_table(which):
+        code = places[...]
+        ends = (jnp.bitwise_and(code, BLOCKS - 1).astype(F32), jnp.right_shift(code, 5).astype(F32))
+        slot_table(ends[which], ends[1 - which], code < BLOCKS * BLOCKS, tables_v[which])
+        move = pltpu.make_async_copy(tables_v[which], tables[which], table_sem.at[which])
+        move.start()
+        return move
+
+    move_table = build_table(0)
+    ridge = []
+    for h in HALVES:
+        column = jnp.zeros((HALF, TILE), F32)
+        for k in range(HALF):
+            column = jnp.where(iota((HALF, TILE), 0) == k, ridge_smem[h * HALF + k], column)
+        ridge.append(column)
     load_targets.wait()
     for b in range(BLOCKS):
         for h in HALVES:
@@ -136,14 +140,14 @@
 
     def product(which, v, h):
         matrix = tiles if which == 0 else tiles_t
-        at = 4 * which
+        table = tables[which]
 
         def body(j, acc):
             for u in range(UNROLL):
                 i = j * UNROLL + u
-                left = jnp.concatenate([v[h][table[at + 1, 2 * i + e]] for e in range(2)], axis=1)
-                right = jnp.concatenate([matrix[table[at, 2 * i + e]] for e in range(2)], axis=0)
-                acc = (acc * table[at + 2, 2 * i].astype(F32)
+                left = jnp.concatenate([v[h][table[1, 2 * i + e]] for e in range(2)], axis=1)
+                right = jnp.concatenate([matrix[table[0, 2 * i + e]] for e in range(2)], axis=0)
+                acc = (acc * table[2, 2 * i].astype(F32)
                        + jnp.dot(left, right, preferred_element_type=F32))
                 prod[h, i] = acc
             return acc
@@ -151,7 +155,7 @@
         lax.fori_loop(0, PAIRS // UNROLL, body, jnp.zeros((HALF, TILE), F32))
 
     def product_block(which, h, b):
-        return prod[h, table[4 * which + 3, b]]
+        return prod[h, tables[which][3, b]]
 
     def wait_bytes(ref, sem):
         pltpu.make_async_copy(ref, ref, sem).wait()
@@ -259,14 +263,18 @@
 
     for h in HALVES:
         product(0, vr0, h)
-    pl.semaphore_wait(barrier, nd + nt - 2)
-    for h in HALVES:
+        if h == 0:
+            pl.semaphore_wait(barrier, nd + nt - 2)
         scatter_g(0, h)
+
+    move_table = build_table(1)
 
     @pl.loop(0, SLOTS // 32)
     def _(j):
         for u in range(32):
             tiles_t[j * 32 + u] = tiles[j * 32 + u].T
+
+    move_table.wait()
 
     p_sq = [nothing, nothing]
     for h in HALVES:
@@ -397,20 +405,15 @@
     vector = pltpu.VMEM((BLOCKS + 1, HALF, TILE), BF16)
     piece = pltpu.VMEM((2, gp, HALF, TILE), F32)
     matrix = pltpu.VMEM((SLOTS, TILE, TILE), BF16)
-    info = jnp.concatenate([
-        tile_row.reshape(1, SLOTS).astype(F32),
-        tile_col.reshape(1, SLOTS).astype(F32),
-        jnp.broadcast_to(tile_count.astype(F32), (1, SLOTS)),
-        jnp.pad(ridge_weight, (0, SLOTS - K)).reshape(1, SLOTS),
-    ], axis=0)
+    live = jnp.arange(SLOTS, dtype=INT).reshape(1, SLOTS) < tile_count
+    places = jnp.where(live, tile_row[0] * BLOCKS + tile_col[0], BLOCKS * BLOCKS)
     results = pl.pallas_call(
         functools.partial(cgls_kernel, nd, nt),
         out_shape=(out, out, out),
-        in_specs=[hbm] * 3,
+        in_specs=[vmem, pl.BlockSpec(memory_space=pltpu.SMEM), hbm, hbm],
         out_specs=(vmem, vmem, vmem),
         scratch_shapes=[
-            pltpu.VMEM((4, SLOTS), F32),
-            pltpu.VMEM((8, PLACES), INT), pltpu.SMEM((8, PLACES), INT),
+            [pltpu.VMEM((4, PLACES), INT)] * 2, [pltpu.SMEM((4, PLACES), INT)] * 2,
             pltpu.VMEM((K, BLOCKS * TILE), F32),
             matrix, matrix,
             pltpu.VMEM((2, PAIRS + 1, HALF, TILE), F32),
@@ -423,15 +426,15 @@
             piece, piece, piece, piece,
             pltpu.VMEM((3, nd, 1, TILE), F32),
             pltpu.VMEM((3, nt, 1, TILE), F32),
-            dma(()), dma(()), dma(()),
+            dma((2,)), dma(()),
             dma((LOADS,)), dma((3, 2)), dma((3, 2)), dma((2, 2)), dma((2, 2)),
             dma((3, 2)), dma((3, 2)), dma((2, 2)), dma((2, 2)),
             dma((3,)), dma((3,)), dma((3,)), dma((3,)),
         ],
         compiler_params=pltpu.CompilerParams(
-            collective_id=0, has_side_effects=True, vmem_limit_bytes=48 * 1024 * 1024),
+            collective_id=0, has_side_effects=True, vmem_limit_bytes=52 * 1024 * 1024),
         name="cgls",
-    )(info, targets, tile_values[0, 0])
+    )(places, ridge_weight, targets, tile_values[0, 0])
     return pl.pallas_call(
         store_kernel,
         out_shape=(out, out, out),

time: 84.4 us -> 82.6 us (0.979)
  local copies, waits for them, and re-layouts: 1.77 us -> 0.65 us
where the time goes in v3:
time: 82.6 us; the launch traced here: 82.2 us
  Pallas kernels  79.6 us (96%)
  between operations  1.29 us (2%)
    pallas_call x1, Pallas kernels, on_device(): pl.pallas_call(functools.partial(cgls_kernel, nd, nt), out_shape=(out, ou...  78.4 us

profile of v3, /device:TPU:2, one launch (start us, length us, event | category | flops | bytes accessed | tf_op | source)
XLA Modules:
  0.0 82.2 jit_solution(8110830743614137864)
XLA Ops:
  1.3 0.7 compare_select_fusion.places
  2.0 0.0 copy-start
  2.0 0.7 copy-done
  2.6 78.4 %cgls.1 = (f32[32,4096]{1,0:T(8,128)S(1)}, f32[32,4096]{1,0:T(8,128)S(1)}, f32[32,4096]{1,0:T(8,128)S(1)}) custom-call(s32[1,256]{1,0:T(1,128)S(1)} %compare_select_fusion.places, f32[32]{0:T(128)S(1)} %copy-done, f32[32,4096]{1,0:T(8,128)} %targets_hbm.1, bf16[256,128,128]{2,1,0:T(8,128)(2,1)} %bitcast.5), custom_call_target="tpu_custom_call" | custom-call | tf_op jit(solution)/shard_map/cgls/pallas_call | solution.py:410
  81.0 1.2 %store.1 = (f32[32,4096]{1,0:T(8,128)}, f32[32,4096]{1,0:T(8,128)}, f32[32,4096]{1,0:T(8,128)}) custom-call(f32[32,4096]{1,0:T(8,128)S(1)} %get-tuple-element.6.x, f32[32,4096]{1,0:T(8,128)S(1)} %get-tuple-element.7.r, f32[32,4096]{1,0:T(8,128)S(1)} %get-tuple-element.8.g), custom_call_target="tpu_custom_call" | custom-call | tf_op jit(solution)/shard_map/store/pallas_call | solution.py:438
Async XLA Ops:
  2.0 0.7 copy-start

commit v4 on v3

--- a/solution.py
+++ b/solution.py
@@ -176,10 +176,10 @@
         return (y * nx + x) * 2 + c
 
     def scatter_g(n, h):
-        for b in range(BLOCKS):
-            send_g[n, h, b] = product_block(0, h, b).astype(BF16)
         for i, o in enumerate(doc_far):
             to = doc_peer(o)
+            for j in range(gp):
+                send_g[n, h, to * gp + j] = product_block(0, h, to * gp + j).astype(BF16)
             pltpu.make_async_remote_copy(
                 src_ref=send_g.at[n, h, pl.ds(to * gp, gp)], dst_ref=recv_g.at[n, h, i],
                 send_sem=gs_sem.at[n, h], recv_sem=gr_sem.at[n, h], device_id={"doc": to}).start()
@@ -204,10 +204,9 @@
         wait_bytes(v[h].at[pl.ds(0, (nd - 1) * gp)], par_sem.at[n, h])
 
     def scatter_q(n, h):
-        for b in range(BLOCKS):
-            send_q[n, h, b] = product_block(1, h, b).astype(BF16)
         for i, o in enumerate(term_far):
             to = term_peer(o)
+            send_q[n, h, to] = product_block(1, h, to).astype(BF16)
             pltpu.make_async_remote_copy(
                 src_ref=send_q.at[n, h, to], dst_ref=recv_q.at[n, h, i],
                 send_sem=qs_sem.at[n, h], recv_sem=qr_sem.at[n, h], device_id={"term": to}).start()
@@ -267,15 +266,15 @@
             pl.semaphore_wait(barrier, nd + nt - 2)
         scatter_g(0, h)
 
+    def transpose(first, count):
+        @pl.loop(first // 32, (first + count) // 32)
+        def _(j):
+            for u in range(32):
+                tiles_t[j * 32 + u] = tiles[j * 32 + u].T
+
     move_table = build_table(1)
-
-    @pl.loop(0, SLOTS // 32)
-    def _(j):
-        for u in range(32):
-            tiles_t[j * 32 + u] = tiles[j * 32 + u].T
-
+    transpose(0, SLOTS // 4)
     move_table.wait()
-
     p_sq = [nothing, nothing]
     for h in HALVES:
         scattered_g(0, h)
@@ -285,6 +284,7 @@
             s_held[h, j] = total
             p_sq[h] = p_sq[h] + total * total
         gather_g(0, h, vp0)
+    transpose(SLOTS // 4, 3 * SLOTS // 4)
 
     for h in HALVES:
         gathered_g(0, h, vp0)

time: 82.6 us -> 82.6 us (level)
  no operation moved by 1% of the time
where the time goes in v4:
time: 82.6 us; the launch traced here: 82.7 us
  Pallas kernels  80 us (97%)
  between operations  1.29 us (2%)
    pallas_call x1, Pallas kernels, on_device(): pl.pallas_call(functools.partial(cgls_kernel, nd, nt), out_shape=(out, ou...  78.8 us

profile of v4, /device:TPU:2, one launch (start us, length us, event | category | flops | bytes accessed | tf_op | source)
XLA Modules:
  0.0 82.7 jit_solution(2480273148313251761)
XLA Ops:
  1.3 0.7 compare_select_fusion.places
  2.0 0.0 copy-start
  2.0 0.7 copy-done
  2.6 78.8 %cgls.1 = (f32[32,4096]{1,0:T(8,128)S(1)}, f32[32,4096]{1,0:T(8,128)S(1)}, f32[32,4096]{1,0:T(8,128)S(1)}) custom-call(s32[1,256]{1,0:T(1,128)S(1)} %compare_select_fusion.places, f32[32]{0:T(128)S(1)} %copy-done, f32[32,4096]{1,0:T(8,128)} %targets_hbm.1, bf16[256,128,128]{2,1,0:T(8,128)(2,1)} %bitcast.5), custom_call_target="tpu_custom_call" | custom-call | tf_op jit(solution)/shard_map/cgls/pallas_call | solution.py:410
  81.5 1.2 %store.1 = (f32[32,4096]{1,0:T(8,128)}, f32[32,4096]{1,0:T(8,128)}, f32[32,4096]{1,0:T(8,128)}) custom-call(f32[32,4096]{1,0:T(8,128)S(1)} %get-tuple-element.6.x, f32[32,4096]{1,0:T(8,128)S(1)} %get-tuple-element.7.r, f32[32,4096]{1,0:T(8,128)S(1)} %get-tuple-element.8.g), custom_call_target="tpu_custom_call" | custom-call | tf_op jit(solution)/shard_map/store/pallas_call | solution.py:438
Async XLA Ops:
  2.0 0.7 copy-start
